TPU v7x, 512 devices: a whole 4x8x8 slice. The times are simulated.
512 devices in a mesh: mode: 2 (over core), oth: 256 (over z, y, x).
Axes of the slice: x: 4, y: 8, z: 8, core: 2. Of those that a mesh axis runs over, the one named last changes fastest.
Arguments:
- tensor: float32 [512, 4, 262144], P('mode', None, 'oth'), may hold values from -20 to 20
- start_basis: float32 [512, 128], replicated, may hold values from -6 to 6
Outputs:
- core_slab: float32 [128, 4, 262144], P('mode', None, 'oth')
- triangle: float32 [512, 512], replicated
All inputs are finite; a program needn't handle non-finite values.
Results may differ from a plain program's by a relative error of at most 0.0003.
Values sent between devices are 32-bit elements; how exact they have to be, the bound alone decides.
A program may use at most 64 MiB of HBM per device.

v0:
```python
import jax
import jax.numpy as jnp
from jax import lax
from jax.sharding import PartitionSpec as P

ITERS = 3


def subspace(triangle, start_basis):
    basis = start_basis
    for sweep in range(ITERS):
        reduced = jnp.dot(
            triangle.T, basis, precision=lax.Precision.HIGHEST, preferred_element_type=jnp.float32
        )
        images = jnp.dot(
            triangle, reduced, precision=lax.Precision.HIGHEST, preferred_element_type=jnp.float32
        )
        gram_small = jnp.dot(
            images.T, images, precision=lax.Precision.HIGHEST, preferred_element_type=jnp.float32
        )
        factor_lower = jnp.linalg.cholesky(gram_small)
        basis = lax.linalg.triangular_solve(
            factor_lower, images, left_side=False, lower=True, transpose_a=True
        )
    return basis


def local(tensor, start_basis):
    rows_local, components, cell_count = tensor.shape
    group_size = lax.axis_size("mode")
    column_total = components * cell_count * lax.axis_size("oth")
    fibers_full = lax.all_to_all(tensor, "mode", split_axis=2, concat_axis=0, tiled=True)
    full_rows = fibers_full.shape[0]
    unfolded = fibers_full.reshape(full_rows, -1)
    covar_part = (
        jnp.dot(
            unfolded,
            unfolded.T,
            precision=lax.Precision.HIGHEST,
            preferred_element_type=jnp.float32,
        )
        / column_total
    )
    flat_part = covar_part.reshape(full_rows * full_rows)
    summed_piece = lax.psum_scatter(flat_part, ("mode", "oth"), scatter_dimension=0, tiled=True)
    summed_covar = lax.all_gather(summed_piece, ("mode", "oth"), axis=0, tiled=True).reshape(
        full_rows, full_rows
    )
    triangle = jnp.linalg.cholesky(summed_covar)
    basis = subspace(triangle, start_basis)
    rank_total = basis.shape[1]
    mode_index = lax.axis_index("mode")
    own_rows = lax.dynamic_slice_in_dim(basis, mode_index * rows_local, rows_local, 0)
    local_unfolded = tensor.reshape(rows_local, -1)
    product = lax.dot_general(
        own_rows,
        local_unfolded,
        (((0,), (0,)), ((), ())),
        precision=lax.Precision.HIGHEST,
        preferred_element_type=jnp.float32,
    )
    core_slab = lax.psum_scatter(
        product.reshape(lax.axis_size("mode") * (rank_total // group_size), components, cell_count),
        "mode",
        scatter_dimension=0,
        tiled=True,
    )
    return (core_slab, triangle)


def solution(mesh):
    return jax.shard_map(
        local,
        mesh=mesh,
        in_specs=(P("mode", None, "oth"), P()),
        out_specs=(P("mode", None, "oth"), P()),
        check_vma=False,
    )
```

profile of v0, /device:TPU:1, one launch (start us, length us, event | category | flops | bytes accessed | tf_op | source)
XLA Modules:
  0.0 643.0 jit_solution(9546581247558276727)
XLA Ops:
  7.2 6.5 %copy.27 = f32[256,4,1024]{0,1,2:T(4,128)} copy(f32[256,4,1024]{2,1,0:T(4,128)} %param.5) | data formatting | bytes 8388608 | tf_op args[0]
  13.8 18.3 %all_to_all.15 = f32[256,4,1024]{0,1,2:T(4,128)} all-to-all(f32[256,4,1024]{0,1,2:T(4,128)} %copy.27), channel_id=1, replica_groups=mesh['mode'=2,'oth'=256] {'mode'}, dimensions={2} | all-to-all | bytes 8388608 | tf_op jit(solution)/shard_map/all_to_all | solution.py:32
  32.1 7.3 %copy.28 = f32[256,4,2,512]{3,1,0,2:T(4,128)} copy(f32[256,4,2,512]{0,1,3,2:T(4,128)} %bitcast.103) | data formatting | bytes 8388608 | tf_op jit(solution)/shard_map/all_to_all | solution.py:32
  39.4 4.1 copy.37
  43.5 6.9 %fusion = f32[64,4,8,128]{3,2,1,0:T(8,128)S(1)} fusion(f32[512,2048]{1,0:T(8,128)S(1)} %bitcast.100), kind=kOutput, calls=%fused_computation.1 | convolution fusion | flops 6442713088 | bytes 5242880 | tf_op jit(solution)/shard_map/dot_general | solution.py:36
  50.4 1.2 copy.38
  51.8 274.5 %all-reduce.4.cloned.1.call-done = f32[262144]{0:T(1024)} async-done(((f32[262144]{0:T(1024)}), f32[262144]{0:T(1024)}) %all-reduce.4.cloned.1.call-update) | async-done | bytes 1048592
  326.3 1.3 dynamic-slice
  327.7 11.7 %reduce-scatter.2.cloned.1.call-start = ((), (), s32[]{:S(2)}) async-start(), calls=%async_computation.2 | async-start | bytes 3145728 | tf_op jit(solution)/shard_map/reduce_scatter | solution.py:62
  339.4 8.0 %copy.39 = f32[32,8,4,1024]{3,1,2,0:T(8,128)} copy(f32[32,8,4,1024]{3,2,1,0:T(4,128)} %bitcast.101) | data formatting | bytes 8388608
  347.3 5.6 copy.34
  352.9 86.7 %all-gather.3.cloned.1.call-done = f32[512,1,512]{2,1,0:T(1,128)} async-done(((f32[1,1,512]{2,1,0:T(1,128)}), f32[512,1,512]{2,1,0:T(1,128)}) %all-gather.3.cloned.1.call-update) | async-done | bytes 1048592 | tf_op jit(solution)/shard_map/all_gather | solution.py:46
  439.6 2.3 copy.29
  442.0 1.4 fusion.1
  443.4 11.7 %cholesky.120 = f32[128,128]{1,0:T(8,128)S(1)} custom-call(f32[128,128]{1,0:T(8,128)S(1)} %cholesky.356), custom_call_target="Cholesky" | custom-call | tf_op jit(solution)/shard_map/jit(cholesky)/cholesky | solution.py:49
  455.2 9.8 %custom-call.32 = f32[1,128,128]{1,2,0:T(8,128)S(1)} custom-call(f32[1,128,128]{2,1,0:T(8,128)S(1)} %get-tuple-element.21), custom_call_target="InvertDiagBlocksLowerTriangular" | custom-call | tf_op jit(solution)/shard_map/jit(cholesky)/cholesky | solution.py:49
  465.8 11.7 %cholesky.244 = f32[128,128]{1,0:T(8,128)S(1)} custom-call(f32[128,128]{1,0:T(8,128)S(1)} %cholesky.360), custom_call_target="Cholesky" | custom-call | tf_op jit(solution)/shard_map/jit(cholesky)/cholesky | solution.py:49
  477.5 10.2 %custom-call.33 = f32[1,128,128]{1,2,0:T(8,128)S(1)} custom-call(f32[1,128,128]{2,1,0:T(8,128)S(1)} %get-tuple-element.18), custom_call_target="InvertDiagBlocksLowerTriangular" | custom-call | tf_op jit(solution)/shard_map/jit(cholesky)/cholesky | solution.py:49
  488.4 11.7 %cholesky.265 = f32[128,128]{1,0:T(8,128)S(1)} custom-call(f32[128,128]{1,0:T(8,128)S(1)} %cholesky.365), custom_call_target="Cholesky" | custom-call | tf_op jit(solution)/shard_map/jit(cholesky)/cholesky | solution.py:49
  500.2 0.7 compare_reduce_fusion.4
  500.8 9.8 %custom-call.34 = f32[1,128,128]{1,2,0:T(8,128)S(1)} custom-call(f32[1,128,128]{2,1,0:T(8,128)S(1)} %get-tuple-element.15), custom_call_target="InvertDiagBlocksLowerTriangular" | custom-call | tf_op jit(solution)/shard_map/jit(cholesky)/cholesky | solution.py:49
  511.2 11.7 %cholesky.282 = f32[128,128]{1,0:T(8,128)S(1)} custom-call(f32[128,128]{1,0:T(8,128)S(1)} %convolution_subtract_fusion.2), custom_call_target="Cholesky" | custom-call | tf_op jit(solution)/shard_map/jit(cholesky)/cholesky | solution.py:49
  523.0 0.7 compare_reduce_fusion.3
  523.6 0.6 compare_reduce_fusion.5
  527.0 2.0 fusion.44
  528.9 1.0 fusion.45
  529.9 0.6 fusion.46
  530.6 11.7 %cholesky.325 = f32[128,128]{1,0:T(8,128)S(1)} custom-call(f32[128,128]{1,0:T(8,128)S(1)} %fusion.21), custom_call_target="Cholesky" | custom-call | tf_op jit(solution)/shard_map/jit(cholesky)/cholesky | solution.py:21
  542.4 0.6 compare_reduce_fusion.2
  543.0 0.7 fusion.11
  543.7 9.8 %custom-call.37 = f32[1,128,128]{1,2,0:T(8,128)S(1)} custom-call(f32[1,128,128]{2,1,0:T(8,128)S(1)} %fusion.11), custom_call_target="InvertDiagBlocksLowerTriangular" | custom-call | tf_op jit(solution)/shard_map/triangular_solve/custom-call.8 | solution.py:22
  553.9 1.8 fusion.47
  555.7 1.2 fusion.48
  557.0 0.6 fusion.49
  557.7 11.7 %cholesky.336 = f32[128,128]{1,0:T(8,128)S(1)} custom-call(f32[128,128]{1,0:T(8,128)S(1)} %fusion.19), custom_call_target="Cholesky" | custom-call | tf_op jit(solution)/shard_map/jit(cholesky)/cholesky | solution.py:21
  569.4 0.6 compare_reduce_fusion.1
  570.1 0.7 fusion.12
  570.7 9.8 %custom-call.38 = f32[1,128,128]{1,2,0:T(8,128)S(1)} custom-call(f32[1,128,128]{2,1,0:T(8,128)S(1)} %fusion.12), custom_call_target="InvertDiagBlocksLowerTriangular" | custom-call | tf_op jit(solution)/shard_map/triangular_solve/custom-call.8 | solution.py:22
  581.0 1.8 fusion.50
  582.8 1.0 fusion.51
  583.8 0.6 fusion.52
  584.5 12.0 %cholesky.347 = f32[128,128]{1,0:T(8,128)S(1)} custom-call(f32[128,128]{1,0:T(8,128)S(1)} %fusion.17), custom_call_target="Cholesky" | custom-call | tf_op jit(solution)/shard_map/jit(cholesky)/cholesky | solution.py:21
  596.5 0.6 compare_reduce_fusion
  597.1 0.7 fusion.13
  597.8 9.8 %custom-call.39 = f32[1,128,128]{1,2,0:T(8,128)S(1)} custom-call(f32[1,128,128]{2,1,0:T(8,128)S(1)} %fusion.13), custom_call_target="InvertDiagBlocksLowerTriangular" | custom-call | tf_op jit(solution)/shard_map/triangular_solve/custom-call.8 | solution.py:22
  608.0 7.8 %fusion.8 = f32[128,4,1024]{2,0,1:T(8,128)} fusion(f32[4,1024,256]{2,1,0:T(8,128)} %bitcast.102, f32[512,128]{0,1:T(8,128)S(1)} %convolution_bitcast_fusion, s32[]{:T(128)S(6)} %select_n.11), kind=kOutput, calls=%fused_computation.20 | convolution fusion | flops 1610612736 | bytes 6422532 | tf_op jit(solution)/shard_map/dot_general | solution.py:55
  615.8 17.3 %reduce-scatter.2.cloned.1.call-done = f32[64,4,1024]{2,0,1:T(8,128)} async-done(((f32[128,4,1024]{2,0,1:T(8,128)}), f32[64,4,1024]{2,0,1:T(8,128)}) %reduce-scatter.2.cloned.1.call-update) | async-done | bytes 1048592 | tf_op jit(solution)/shard_map/reduce_scatter | solution.py:62
  633.1 2.9 copy.35
  (36 shorter events, 4.1 us)
Async XLA Ops:
  7.2 519.8 %copy-start = (f32[512,128]{1,0:T(8,128)S(1)}, f32[512,128]{1,0:T(8,128)}, u32[]{:S(2)}) copy-start(f32[512,128]{1,0:T(8,128)} %param.6) | copy-start | bytes 786436
  7.2 319.1 %all-reduce.4.cloned.1.call-start = ((), (), s32[]{:S(2)}) async-start(), calls=%async_computation.4 | async-start | bytes 2097152
  51.7 387.9 %all-gather.3.cloned.1.call-start = ((), (), s32[]{:S(2)}) async-start(), calls=%async_computation.3 | async-start | bytes 1050624 | tf_op jit(solution)/shard_map/all_gather | solution.py:46
  327.7 305.5 %reduce-scatter.2.cloned.1.call-start = ((), (), s32[]{:S(2)}) async-start(), calls=%async_computation.2 | async-start | bytes 3145728 | tf_op jit(solution)/shard_map/reduce_scatter | solution.py:62
  526.9 55.8 %copy-start.1 = (f32[512,512]{1,0:T(8,128)}, f32[512,512]{1,0:T(8,128)S(1)}, u32[]{:S(2)}) copy-start(f32[512,512]{1,0:T(8,128)S(1)} %select_select_fusion) | copy-start | bytes 3145732
Sparse Core Ops, SparseCore 0:
  51.8 274.4 all-reduce.3
  331.1 108.5 all-gather.2
  616.0 17.1 reduce-scatter.1
where the time goes:
time: 651 us; the launch traced here: 643 us
  waiting for transfers between devices  379 us (58%)
  other arithmetic  149 us (23%)
  local copies, waits for them, and re-layouts  39.7 us (6%)
  matrix products  28.3 us (4%)
  blocking collectives  18.3 us (3%)
  between operations  17 us (3%)
  starting transfers between devices  11.8 us (2%)
    unnamed x4, waiting for transfers between devices  275 us
    all_gather x1, waiting for transfers between devices, local(): lax.all_gather(summed_piece, ('mode', 'oth'), axis=0, tiled=True)  86.7 us
    another operation x14, other arithmetic, local(): triangle = jnp.linalg.cholesky(summed_covar)  78.8 us
    another operation x9, other arithmetic, subspace(): factor_lower = jnp.linalg.cholesky(gram_small)  37.4 us
    another operation x6, other arithmetic, subspace(): lax.linalg.triangular_solve(factor_lower, images, left_side=False, lower=...  31.4 us
    unnamed x10, local copies, waits for them, and re-layouts  24.1 us
    all_to_all x1, blocking collectives, local(): lax.all_to_all(tensor, 'mode', split_axis=2, concat_axis=0, tiled=True)  18.3 us
    reduce_scatter x1, waiting for transfers between devices, local(): lax.psum_scatter(product.reshape(lax.axis_size('mode') * (rank_total // g...  17.3 us
  transfers between devices with their start and end apart: 3, of which 3 were waited for; matrix products, arithmetic and copies ran while one was open for 2% of the time, Pallas kernels for 0%

commit v1 on v0

v1 whole, which is shorter than its diff:
```python
import jax
import jax.numpy as jnp
from jax import lax
from jax.experimental import pallas as pl
from jax.experimental.pallas import tpu as pltpu
from jax.sharding import PartitionSpec as P

ITERS = 3
T = 128
XS, YS, ZS = 4, 8, 8
HIGH = lax.Precision.HIGHEST


def sum_kernel(diag, cross, out, work, half_in, in1, in2, in3, send_sem, recv_sem):
    mode = lax.axis_index("mode")
    oth = lax.axis_index("oth")
    x = lax.rem(oth, XS)
    y = lax.rem(oth // XS, YS)
    z = oth // (XS * YS)
    rows = work.shape[0]
    part = rows // 2
    piece = part // ZS
    own = cross.shape[0] // 2
    base = rows - own
    other = {"mode": 1 - mode, "oth": oth}

    def along(axis, place):
        if axis == "z":
            cell = place * (XS * YS) + y * XS + x
        elif axis == "y":
            cell = z * (XS * YS) + place * XS + x
        else:
            cell = z * (XS * YS) + y * XS + place
        return {"mode": mode, "oth": cell}

    size = {"x": XS, "y": YS, "z": ZS}
    here = {"x": x, "y": y, "z": z}

    def peer(axis, step):
        return lax.rem(here[axis] + step, size[axis])

    barrier = pltpu.get_barrier_semaphore()
    pl.semaphore_signal(barrier, inc=1, device_id=other)
    count = 1
    for axis in "zyx":
        for step in range(1, size[axis]):
            pl.semaphore_signal(barrier, inc=1, device_id=along(axis, peer(axis, step)))
            count += 1
    pl.semaphore_wait(barrier, count)

    def copy(src, dst, slot, device):
        return pltpu.make_async_remote_copy(
            src_ref=src,
            dst_ref=dst,
            send_sem=send_sem.at[slot],
            recv_sem=recv_sem.at[slot],
            device_id=device,
        )

    pending = []
    first = copy(
        cross.at[pl.ds(pl.multiple_of((1 - mode) * own, 8), own)], half_in, 0, other
    )
    first.start()
    work[:base] = diag[...]
    first.wait_recv()
    work[base:] = cross[pl.ds(pl.multiple_of(mode * own, 8), own)] + half_in[...]
    pending.append(first)

    plans = (("z", "y"), ("y", "z"))
    slot = 1
    stage = []
    for index, (major, minor) in enumerate(plans):
        for step in range(1, size[major]):
            to = peer(major, step)
            start = pl.multiple_of(index * part + to * piece, 8)
            item = copy(
                work.at[pl.ds(start, piece)], in1.at[index, here[major]], slot, along(major, to)
            )
            item.start()
            stage.append(item)
            slot += 1
    for index, (major, minor) in enumerate(plans):
        start = pl.multiple_of(index * part + here[major] * piece, 8)
        in1[index, here[major]] = work[pl.ds(start, piece)]
    position = 0
    second = []
    for index, (major, minor) in enumerate(plans):
        for step in range(1, size[major]):
            stage[position].wait_recv()
            position += 1
        total = in1[index, 0]
        for place in range(1, size[major]):
            total = total + in1[index, place]
        in2[index, here[minor]] = total
        for step in range(1, size[minor]):
            spot = in2.at[index, here[minor]]
            item = copy(spot, spot, slot, along(minor, peer(minor, step)))
            item.start()
            second.append(item)
            slot += 1
    pending += stage
    position = 0
    third = []
    for index, (major, minor) in enumerate(plans):
        for step in range(1, size[minor]):
            second[position].wait_recv()
            position += 1
        total = in2[index, 0]
        for place in range(1, size[minor]):
            total = total + in2[index, place]
        in3[index, x] = total
        for step in range(1, XS):
            spot = in3.at[index, x]
            item = copy(spot, spot, slot, along("x", peer("x", step)))
            item.start()
            third.append(item)
            slot += 1
    pending += second
    position = 0
    fourth = []
    passed = []
    for index, (major, minor) in enumerate(plans):
        for step in range(1, XS):
            third[position].wait_recv()
            position += 1
        total = in3[index, 0]
        for place in range(1, XS):
            total = total + in3[index, place]
        start = pl.multiple_of(index * part + here[major] * piece, 8)
        out[mode, pl.ds(start, piece)] = total
        spot = out.at[mode, pl.ds(start, piece)]
        for step in range(1, size[major]):
            item = copy(spot, spot, slot, along(major, peer(major, step)))
            item.start()
            fourth.append(item)
            slot += 1
        item = copy(spot, spot, slot, other)
        item.start()
        passed.append(item)
        slot += 1
    pending += third
    position = 0
    for index, (major, minor) in enumerate(plans):
        for step in range(1, size[major]):
            fourth[position].wait_recv()
            position += 1
            source = lax.rem(here[major] + (size[major] - step), size[major])
            start = pl.multiple_of(index * part + source * piece, 8)
            spot = out.at[mode, pl.ds(start, piece)]
            item = copy(spot, spot, slot, other)
            item.start()
            passed.append(item)
            slot += 1
    pending += fourth
    for item in passed:
        item.wait_recv()
    pending += passed
    for item in pending:
        item.wait_send()


def summed(diag, cross):
    rows = diag.shape[0] + cross.shape[0] // 2
    piece = rows // 2 // ZS
    copies = 1 + 14 + 14 + 6 + 14 + 2 + 14
    return pl.pallas_call(
        sum_kernel,
        out_shape=jax.ShapeDtypeStruct((2, rows, T), jnp.float32),
        in_specs=[pl.BlockSpec(memory_space=pltpu.VMEM)] * 2,
        out_specs=pl.BlockSpec(memory_space=pltpu.VMEM),
        scratch_shapes=[
            pltpu.VMEM((rows, T), jnp.float32),
            pltpu.VMEM((cross.shape[0] // 2, T), jnp.float32),
            pltpu.VMEM((2, ZS, piece, T), jnp.float32),
            pltpu.VMEM((2, ZS, piece, T), jnp.float32),
            pltpu.VMEM((2, XS, piece, T), jnp.float32),
            pltpu.SemaphoreType.DMA((copies,)),
            pltpu.SemaphoreType.DMA((copies,)),
        ],
        compiler_params=pltpu.CompilerParams(collective_id=0, has_side_effects=True),
        name="covariance_sum",
    )(diag, cross)


def dot(a, b, ca, cb):
    return lax.dot_general(
        a, b, (((ca,), (cb,)), ((), ())), precision=HIGH, preferred_element_type=jnp.float32
    )


def factor(mats, uppers):
    groups = T // 8
    lane = lax.broadcasted_iota(jnp.int32, (8, T), 1)
    sub = lax.broadcasted_iota(jnp.int32, (8, T), 0)

    def body(k, state):
        new_state = []
        for mat, upper in zip(state, uppers):
            mat = list(mat)
            done = jnp.zeros((8, T), jnp.float32)
            for i in range(8):
                row = jnp.broadcast_to(mat[0][i : i + 1, :], (8, T))
                pivot = jnp.broadcast_to(row[:, i : i + 1], (8, T))
                inv = lax.rsqrt(pivot)
                at = lane == i
                row_one = jnp.where(at, 1.0, row)
                scaled = row_one * (inv * inv)
                done = jnp.where(sub == i, row * inv, done)
                for g in range(groups):
                    col = jnp.broadcast_to(mat[g][:, i : i + 1], (8, T))
                    if g == 0:
                        col = jnp.where(sub > i, col, 0.0)
                    else:
                        col = jnp.where(g + k < groups, col, 0.0)
                    mat[g] = jnp.where(at, 0.0, mat[g]) - col * scaled
                mat[0] = jnp.where(sub == i, row_one * inv, mat[0])
            upper[pl.ds(pl.multiple_of(k * 8, 8), 8), :] = pltpu.roll(done, k * 8, axis=1)
            mat = [pltpu.roll(m, T - 8, axis=1) for m in mat]
            new_state.append(tuple(mat[1:] + mat[:1]))
        return tuple(new_state)

    state = tuple(tuple(m[8 * g : 8 * g + 8, :] for g in range(groups)) for m in mats)
    state = lax.fori_loop(0, groups, body, state)
    row = lax.broadcasted_iota(jnp.int32, (T, T), 0)
    col = lax.broadcasted_iota(jnp.int32, (T, T), 1)
    inverses = [jnp.where(row >= col, jnp.concatenate(s, axis=0), 0.0) for s in state]
    lowers = [jnp.where(row <= col, u[...], 0.0).T for u in uppers]
    return lowers, inverses


PLACES = (((0, 0), (1, 0), (1, 1), (2, 0), (2, 1)), ((2, 2), (3, 2), (3, 3), (3, 0), (3, 1)))


def small_kernel(scale, sums, start, triangle, basis_out, covar, work, images, upper1, upper2):
    blocks = covar.shape[0] // T
    for m in range(2):
        for b, (r, c) in enumerate(PLACES[m]):
            block = sums[m, b] * scale
            covar[r * T : r * T + T, c * T : c * T + T] = block
            work[r * T : r * T + T, c * T : c * T + T] = block
            if r != c:
                covar[c * T : c * T + T, r * T : r * T + T] = block.T
    basis_out[...] = start[...]
    for r in range(blocks):
        lo = r * T
        mats = [work[lo : lo + T, lo : lo + T]]
        uppers = [upper1]
        if r < ITERS:
            images[...] = dot(covar[...], basis_out[...], 1, 0)
            mats.append(dot(images[...], images[...], 0, 0))
            uppers.append(upper2)
        lowers, inverses = factor(mats, uppers)
        triangle[lo : lo + T, lo : lo + T] = lowers[0]
        if r < ITERS:
            basis_out[...] = dot(images[...], inverses[1], 1, 1)
        if r > 0:
            triangle[:lo, lo : lo + T] = jnp.zeros((lo, T), jnp.float32)
        if r < blocks - 1:
            panel = dot(work[lo + T :, lo : lo + T], inverses[0], 1, 1)
            triangle[lo + T :, lo : lo + T] = panel
            for c in range(r + 1, blocks):
                top = c * T
                work[top:, top : top + T] = work[top:, top : top + T] - dot(
                    panel[top - lo - T :, :], panel[top - lo - T : top - lo, :], 1, 1
                )


def small(scale, sums, start_basis):
    n, rank = start_basis.shape
    return pl.pallas_call(
        lambda *refs: small_kernel(scale, *refs),
        out_shape=[
            jax.ShapeDtypeStruct((n, n), jnp.float32),
            jax.ShapeDtypeStruct((n, rank), jnp.float32),
        ],
        in_specs=[pl.BlockSpec(memory_space=pltpu.VMEM)] * 2,
        out_specs=[pl.BlockSpec(memory_space=pltpu.VMEM)] * 2,
        scratch_shapes=[
            pltpu.VMEM((n, n), jnp.float32),
            pltpu.VMEM((n, n), jnp.float32),
            pltpu.VMEM((n, rank), jnp.float32),
            pltpu.VMEM((T, T), jnp.float32),
            pltpu.VMEM((T, T), jnp.float32),
        ],
        name="factors",
    )(sums, start_basis)


def local(tensor, start_basis):
    rows, components, cells = tensor.shape
    total = components * cells * lax.axis_size("oth")
    mode = lax.axis_index("mode")
    swap = [(0, 1), (1, 0)]
    half = cells // 2
    away = lax.dynamic_slice_in_dim(tensor, (1 - mode) * half, half, 2)
    kept = lax.dynamic_slice_in_dim(tensor, mode * half, half, 2)
    arrived = lax.ppermute(away, "mode", swap)
    both = (((1, 2), (1, 2)), ((), ()))
    own = lax.dot_general(tensor, tensor, both, precision=HIGH, preferred_element_type=jnp.float32)
    mixed = lax.dot_general(kept, arrived, both, precision=HIGH, preferred_element_type=jnp.float32)
    mixed = jnp.where(mode == 0, mixed.T, mixed)
    diag = jnp.concatenate([own[:T, :T], own[T:, :T], own[T:, T:]], axis=0)
    cross = jnp.concatenate([mixed[:T, :T], mixed[:T, T:], mixed[T:, :T], mixed[T:, T:]], axis=0)
    sums = summed(diag, cross).reshape(2, -1, T, T)
    triangle, basis = small(1.0 / total, sums, start_basis)
    rank = basis.shape[1] // 2
    own_rows = lax.dynamic_slice_in_dim(basis, mode * rows, rows, 0)
    given = lax.dynamic_slice_in_dim(own_rows, (1 - mode) * rank, rank, 1)
    mine = lax.dynamic_slice_in_dim(own_rows, mode * rank, rank, 1)
    first = (((0,), (0,)), ((), ()))
    sent = lax.ppermute(
        lax.dot_general(given, tensor, first, precision=HIGH, preferred_element_type=jnp.float32),
        "mode",
        swap,
    )
    stays = lax.dot_general(mine, tensor, first, precision=HIGH, preferred_element_type=jnp.float32)
    return (stays + sent, triangle)


def solution(mesh):
    return jax.shard_map(
        local,
        mesh=mesh,
        in_specs=(P("mode", None, "oth"), P()),
        out_specs=(P("mode", None, "oth"), P()),
        check_vma=False,
    )
```

time: 651 us -> 223 us (0.34); the launches traced: 643 us -> 222 us
  waiting for transfers between devices: 379 us -> 2.32 us
  Pallas kernels: 0 us -> 161 us
  other arithmetic: 149 us -> 1.45 us
  local copies, waits for them, and re-layouts: 39.7 us -> 11.5 us
  blocking collectives: 18.3 us -> 0 us
  between operations: 17 us -> 0.74 us
    unnamed x4 -> x0, waiting for transfers between devices: 275 us -> none
    pallas_call x0 -> x2, Pallas kernels: none -> 161 us  [the longest x1 122 us: small(): pl.pallas_call(lambda *refs: small_kernel(scale, *refs), out_shape=[jax.S...]
    another operation x29 -> x0, other arithmetic: 148 us -> none  [the longest x14 78.8 us: local(): triangle = jnp.linalg.cholesky(summed_covar)]
    all_gather x1 -> x0, waiting for transfers between devices: 86.7 us -> none  [local(): lax.all_gather(summed_piece, ('mode', 'oth'), axis=0, tiled=True)]
    all_to_all x1 -> x0, blocking collectives: 18.3 us -> none  [local(): lax.all_to_all(tensor, 'mode', split_axis=2, concat_axis=0, tiled=True)]
    reduce_scatter x1 -> x0, waiting for transfers between devices: 17.3 us -> none  [local(): lax.psum_scatter(product.reshape(lax.axis_size('mode') * (rank_total // g...]
    unnamed x10 -> x4, local copies, waits for them, and re-layouts: 24.1 us -> 8.21 us
    reduce_scatter x1 -> x0, starting transfers between devices: 11.7 us -> none  [local(): lax.psum_scatter(product.reshape(lax.axis_size('mode') * (rank_total // g...]
  transfers between devices with their start and end apart: 3 -> 2, of which waited for: 3 -> 1; matrix products, arithmetic and copies ran while one was open for 2% -> 8% of each run, Pallas kernels for 0% -> 0%
where the time goes in v1:
time: 223 us; the launch traced here: 222 us
  Pallas kernels  161 us (72%)
  matrix products  34.6 us (16%)
  local copies, waits for them, and re-layouts  11.5 us (5%)
  starting transfers between devices  11.1 us (5%)
  waiting for transfers between devices  2.32 us (1%)
    pallas_call x1, Pallas kernels, small(): pl.pallas_call(lambda *refs: small_kernel(scale, *refs), out_shape=[jax.S...  122 us
    pallas_call x1, Pallas kernels, summed(): pl.pallas_call(sum_kernel, out_shape=jax.ShapeDtypeStruct((2, rows, T), j...  38.3 us
    dot_general x1, matrix products, local(): lax.dot_general(tensor, tensor, both, precision=HIGH, preferred_element_t...  16.9 us
    ppermute x1, starting transfers between devices, local(): arrived = lax.ppermute(away, 'mode', swap)  8.91 us
    unnamed x4, local copies, waits for them, and re-layouts  8.21 us
    dot_general x1, matrix products, local(): lax.dot_general(given, tensor, first, precision=HIGH, preferred_element_t...  7.14 us
    dot_general x1, matrix products, local(): lax.dot_general(mine, tensor, first, precision=HIGH, preferred_element_ty...  7.05 us
  transfers between devices with their start and end apart: 2, of which 1 were waited for; matrix products, arithmetic and copies ran while one was open for 8% of the time, Pallas kernels for 0%

profile of v1, /device:TPU:1, one launch (start us, length us, event | category | flops | bytes accessed | tf_op | source)
XLA Modules:
  0.0 222.2 jit_solution(16588763483495125448)
XLA Ops:
  0.6 6.6 %copy.4 = f32[256,4,1024]{2,0,1:T(8,128)} copy(f32[256,4,1024]{2,1,0:T(4,128)} %param.2) | data formatting | bytes 8388608 | tf_op args[0]
  7.2 3.1 %constant_dynamic-slice_fusion = f32[256,4,512]{2,0,1:T(8,128)} fusion(f32[256,4,1024]{2,0,1:T(8,128)} %copy.4, s32[]{:T(128)S(6)} %select_n.31), kind=kLoop, calls=%fused_computation.13 | loop fusion | bytes 4194308 | tf_op jit(solution)/shard_map/dynamic_slice | solution.py:296
  10.3 8.9 %collective-permute-start = (f32[256,4,512]{2,0,1:T(8,128)}, f32[256,4,512]{2,0,1:T(8,128)S(1)}, u32[]{:S(2)}, u32[]{:S(2)}) collective-permute-start(f32[256,4,512]{2,0,1:T(8,128)} %constant_dynamic-slice_fusion), channel_id=1, source_target_pairs={{0,256},{256,0},{1,257},{257,1},{2,258},{258,2},{3,259},{259,3},{4... | collective-permute-start | bytes 6291464 | tf_op jit(solution)/shard_map/ppermute | solution.py:298
  19.2 16.9 %convolution_bitcast_fusion = f32[256,256]{1,0:T(8,128)S(1)} fusion(f32[256,4,1024]{2,1,0:T(4,128)} %param.2), kind=kOutput, calls=%fused_computation.3 | convolution fusion | flops 3221225472 | bytes 4456448 | tf_op jit(solution)/shard_map/dot_general | solution.py:300
  36.2 0.7 pad_maximum_fusion.1.diag
  36.9 0.0 collective-permute-done
  36.9 3.5 %fusion.2 = f32[256,256]{1,0:T(8,128)S(1)} fusion(f32[256,4,512]{2,0,1:T(8,128)S(1)} %collective-permute-done, f32[256,4,1024]{2,0,1:T(8,128)} %copy.4, s32[]{:T(128)S(6)} %select_n.30), kind=kOutput, calls=%fused_computation.4 | convolution fusion | flops 1610612736 | bytes 4456452 | tf_op jit(solution)/shard_map/dot_general | solution.py:301
  40.4 0.1 copy.8
  40.6 0.7 pad_maximum_fusion.cross
  41.3 38.3 %covariance_sum.1 = f32[2,640,128]{2,1,0:T(8,128)} custom-call(f32[384,128]{1,0:T(8,128)} %pad_maximum_fusion.1.diag, f32[512,128]{1,0:T(8,128)} %pad_maximum_fusion.cross), custom_call_target="tpu_custom_call" | custom-call | tf_op jit(solution)/shard_map/covariance_sum/pallas_call | solution.py:167
  79.6 122.2 %factors.1 = (f32[512,512]{1,0:T(8,128)}, f32[512,128]{1,0:T(8,128)}) custom-call(f32[2,5,128,128]{3,2,1,0:T(8,128)} %bitcast.14, f32[512,128]{1,0:T(8,128)} %refs_1_.1), custom_call_target="tpu_custom_call" | custom-call | tf_op jit(solution)/shard_map/factors/pallas_call | solution.py:271
  201.8 0.0 copy-start
  201.8 7.1 %fusion.5 = f32[64,4,1024]{2,0,1:T(8,128)S(1)} fusion(f32[512,128]{1,0:T(8,128)} %get-tuple-element.4, s32[]{:T(128)S(6)} %select_n.34, s32[]{:T(128)S(6)} %select_n.38, f32[256,4,1024]{2,1,0:T(4,128)} %param.2), kind=kOutput, calls=%fused_computation.8 | convolution fusion | flops 805306368 | bytes 5373960 | tf_op jit(solution)/shard_map/dot_general | solution.py:313
  209.0 2.2 collective-permute-start.1
  211.2 2.3 %collective-permute-done.1 = f32[64,4,1024]{2,0,1:T(8,128)S(1)} collective-permute-done((f32[64,4,1024]{2,0,1:T(8,128)S(1)}, f32[64,4,1024]{2,0,1:T(8,128)S(1)}, u32[]{:S(2)}, u32[]{:S(2)}) %collective-permute-start.1) | collective-permute-done | bytes 1048608 | tf_op jit(solution)/shard_map/ppermute | solution.py:312
  213.5 0.0 copy-done
  213.5 7.1 %convolution_add_fusion = f32[64,4,1024]{2,0,1:T(8,128)S(1)} fusion(f32[64,4,1024]{2,0,1:T(8,128)S(1)} %collective-permute-done.1, f32[512,128]{1,0:T(8,128)S(1)} %copy-done, s32[]{:T(128)S(6)} %select_n.34, s32[]{:T(128)S(6)} %select_n.36, f32[256,4,1024]{2,1,0:T(4,128)} %param.2), kind=kOutput, calls=%fused_computation.2 | convolution fusion | flops 805568512 | bytes 6422536 | tf_op jit(solution)/shard_map/dot_general | solution.py:317
  220.6 1.7 copy.13
  (4 shorter events, 0.1 us)
Async XLA Ops:
  10.3 26.6 %collective-permute-start = (f32[256,4,512]{2,0,1:T(8,128)}, f32[256,4,512]{2,0,1:T(8,128)S(1)}, u32[]{:S(2)}, u32[]{:S(2)}) collective-permute-start(f32[256,4,512]{2,0,1:T(8,128)} %constant_dynamic-slice_fusion), channel_id=1, source_target_pairs={{0,256},{256,0},{1,257},{257,1},{2,258},{258,2},{3,259},{259,3},{4... | collective-permute-start | bytes 6291464 | tf_op jit(solution)/shard_map/ppermute | solution.py:298
  201.8 11.7 %copy-start = (f32[512,128]{1,0:T(8,128)S(1)}, f32[512,128]{1,0:T(8,128)}, u32[]{:S(2)}) copy-start(f32[512,128]{1,0:T(8,128)} %get-tuple-element.4) | copy-start | bytes 786436
  209.0 4.5 %collective-permute-start.1 = (f32[64,4,1024]{2,0,1:T(8,128)S(1)}, f32[64,4,1024]{2,0,1:T(8,128)S(1)}, u32[]{:S(2)}, u32[]{:S(2)}) collective-permute-start(f32[64,4,1024]{2,0,1:T(8,128)S(1)} %fusion.5), channel_id=1, source_target_pairs={{0,256},{256,0},{1,257},{257,1},{2,258},{258,2},{3,259},{259,3},{4... | collective-permute-start | bytes 3145736 | tf_op jit(solution)/shard_map/ppermute | solution.py:312

commit v2 on v1

--- a/solution.py
+++ b/solution.py
@@ -189,42 +189,82 @@
     )
 
 
+def thirds(x):
+    high = x.astype(jnp.bfloat16).astype(jnp.float32)
+    rest = x - high
+    middle = rest.astype(jnp.bfloat16).astype(jnp.float32)
+    return high, middle, rest - middle
+
+
+def outer(a, b):
+    ah, am, al = thirds(a)
+    bh, bm, bl = thirds(b)
+    left = jnp.concatenate([ah, ah, am, am, ah, al], axis=0).astype(jnp.bfloat16)
+    right = jnp.concatenate([bh, bm, bh, bm, bl, bh], axis=0).astype(jnp.bfloat16)
+    return lax.dot_general(
+        left, right, (((0,), (0,)), ((), ())), preferred_element_type=jnp.float32
+    )
+
+
 def factor(mats, uppers):
     groups = T // 8
     lane = lax.broadcasted_iota(jnp.int32, (8, T), 1)
     sub = lax.broadcasted_iota(jnp.int32, (8, T), 0)
 
+    def spread(v, i):
+        return jnp.broadcast_to(v[i : i + 1, :], (8, T))
+
+    def column(v, i):
+        return jnp.broadcast_to(v[:, i : i + 1], (8, T))
+
     def body(k, state):
         new_state = []
-        for mat, upper in zip(state, uppers):
+        keep = lane < jnp.where(k == 0, T, T - 8)
+        more = k < groups - 1
+        active = (lane >= 8) & (lane < T - 8 * k)
+        for (mat, left, right), upper in zip(state, uppers):
             mat = list(mat)
+            late = outer(left, right)
+            for g in range(1, groups - 1):
+                mat[g] = jnp.where(keep, mat[g], 0.0) - late[8 * g : 8 * g + 8, :]
+            head, following = mat[0], mat[1]
+            heads = [column(head, i) for i in range(8)]
+            nexts = [jnp.where(more, column(following, i), 0.0) for i in range(8)]
             done = jnp.zeros((8, T), jnp.float32)
             for i in range(8):
-                row = jnp.broadcast_to(mat[0][i : i + 1, :], (8, T))
-                pivot = jnp.broadcast_to(row[:, i : i + 1], (8, T))
-                inv = lax.rsqrt(pivot)
+                row = spread(head, i)
+                inv = lax.rsqrt(spread(heads[i], i))
+                square = inv * inv
                 at = lane == i
                 row_one = jnp.where(at, 1.0, row)
-                scaled = row_one * (inv * inv)
+                scaled = row_one * square
                 done = jnp.where(sub == i, row * inv, done)
-                for g in range(groups):
-                    col = jnp.broadcast_to(mat[g][:, i : i + 1], (8, T))
-                    if g == 0:
-                        col = jnp.where(sub > i, col, 0.0)
-                    else:
-                        col = jnp.where(g + k < groups, col, 0.0)
-                    mat[g] = jnp.where(at, 0.0, mat[g]) - col * scaled
-                mat[0] = jnp.where(sub == i, row_one * inv, mat[0])
+                below = jnp.where(sub > i, heads[i], 0.0)
+                for j in range(i + 1, 8):
+                    factor_j = spread(heads[j], i) * square
+                    heads[j] = heads[j] - below * factor_j
+                    nexts[j] = nexts[j] - nexts[i] * factor_j
+                head = jnp.where(at, 0.0, head) - below * scaled
+                head = jnp.where(sub == i, row_one * inv, head)
+                following = jnp.where(at, 0.0, following) - nexts[i] * scaled
             upper[pl.ds(pl.multiple_of(k * 8, 8), 8), :] = pltpu.roll(done, k * 8, axis=1)
+            left = jnp.where(active, head, 0.0)
+            right = jnp.where((lane < 8) & (lane > sub), 0.0, head)
+            mat = [head, following] + mat[2:]
             mat = [pltpu.roll(m, T - 8, axis=1) for m in mat]
-            new_state.append(tuple(mat[1:] + mat[:1]))
+            left = pltpu.roll(left, T - 8, axis=1)
+            right = pltpu.roll(right, T - 8, axis=1)
+            new_state.append((tuple(mat[1:] + mat[:1]), left, right))
         return tuple(new_state)
 
-    state = tuple(tuple(m[8 * g : 8 * g + 8, :] for g in range(groups)) for m in mats)
+    zero = jnp.zeros((8, T), jnp.float32)
+    state = tuple(
+        (tuple(m[8 * g : 8 * g + 8, :] for g in range(groups)), zero, zero) for m in mats
+    )
     state = lax.fori_loop(0, groups, body, state)
     row = lax.broadcasted_iota(jnp.int32, (T, T), 0)
     col = lax.broadcasted_iota(jnp.int32, (T, T), 1)
-    inverses = [jnp.where(row >= col, jnp.concatenate(s, axis=0), 0.0) for s in state]
+    inverses = [jnp.where(row >= col, jnp.concatenate(s[0], axis=0), 0.0) for s in state]
     lowers = [jnp.where(row <= col, u[...], 0.0).T for u in uppers]
     return lowers, inverses
 
@@ -232,7 +272,9 @@
 PLACES = (((0, 0), (1, 0), (1, 1), (2, 0), (2, 1)), ((2, 2), (3, 2), (3, 3), (3, 0), (3, 1)))
 
 
-def small_kernel(scale, sums, start, triangle, basis_out, covar, work, images, upper1, upper2):
+def small_kernel(
+    scale, sums, start, triangle, basis_turned, covar, work, images, basis, upper1, upper2
+):
     blocks = covar.shape[0] // T
     for m in range(2):
         for b, (r, c) in enumerate(PLACES[m]):
@@ -241,19 +283,21 @@
             work[r * T : r * T + T, c * T : c * T + T] = block
             if r != c:
                 covar[c * T : c * T + T, r * T : r * T + T] = block.T
-    basis_out[...] = start[...]
+    basis[...] = start[...]
     for r in range(blocks):
         lo = r * T
         mats = [work[lo : lo + T, lo : lo + T]]
         uppers = [upper1]
         if r < ITERS:
-            images[...] = dot(covar[...], basis_out[...], 1, 0)
+            images[...] = dot(covar[...], basis[...], 1, 0)
             mats.append(dot(images[...], images[...], 0, 0))
             uppers.append(upper2)
         lowers, inverses = factor(mats, uppers)
         triangle[lo : lo + T, lo : lo + T] = lowers[0]
-        if r < ITERS:
-            basis_out[...] = dot(images[...], inverses[1], 1, 1)
+        if r < ITERS - 1:
+            basis[...] = dot(images[...], inverses[1], 1, 1)
+        elif r == ITERS - 1:
+            basis_turned[...] = dot(inverses[1], images[...], 1, 1)
         if r > 0:
             triangle[:lo, lo : lo + T] = jnp.zeros((lo, T), jnp.float32)
         if r < blocks - 1:
@@ -272,7 +316,7 @@
         lambda *refs: small_kernel(scale, *refs),
         out_shape=[
             jax.ShapeDtypeStruct((n, n), jnp.float32),
-            jax.ShapeDtypeStruct((n, rank), jnp.float32),
+            jax.ShapeDtypeStruct((rank, n), jnp.float32),
         ],
         in_specs=[pl.BlockSpec(memory_space=pltpu.VMEM)] * 2,
         out_specs=[pl.BlockSpec(memory_space=pltpu.VMEM)] * 2,
@@ -280,6 +324,7 @@
             pltpu.VMEM((n, n), jnp.float32),
             pltpu.VMEM((n, n), jnp.float32),
             pltpu.VMEM((n, rank), jnp.float32),
+            pltpu.VMEM((n, rank), jnp.float32),
             pltpu.VMEM((T, T), jnp.float32),
             pltpu.VMEM((T, T), jnp.float32),
         ],
@@ -287,35 +332,173 @@
     )(sums, start_basis)
 
 
+def partner():
+    mode = lax.axis_index("mode")
+    return mode, {"mode": 1 - mode, "oth": lax.axis_index("oth")}
+
+
+def greet(other):
+    barrier = pltpu.get_barrier_semaphore()
+    pl.semaphore_signal(barrier, inc=1, device_id=other)
+    pl.semaphore_wait(barrier, 1)
+
+
+def pair_kernel(
+    tensor, diag, cross, arrived, whole, got, square, mixed, load_sem, send_sem, recv_sem, store_sem
+):
+    mode, other = partner()
+    fields, rows, cells = whole.shape
+    half = cells // 2
+    kept = pl.ds(pl.multiple_of(mode * half, T), half)
+    away = pl.ds(pl.multiple_of((1 - mode) * half, T), half)
+
+    def load(c):
+        return pltpu.make_async_copy(tensor.at[:, c, :], whole.at[c], load_sem.at[c])
+
+    def send(c):
+        return pltpu.make_async_remote_copy(
+            src_ref=whole.at[c, :, away],
+            dst_ref=got.at[c],
+            send_sem=send_sem.at[c],
+            recv_sem=recv_sem.at[c],
+            device_id=other,
+        )
+
+    def store(c):
+        return pltpu.make_async_copy(got.at[c], arrived.at[c], store_sem.at[c])
+
+    for c in range(fields):
+        load(c).start()
+    greet(other)
+    for c in range(fields):
+        load(c).wait()
+        send(c).start()
+    square[...] = jnp.zeros_like(square)
+    mixed[...] = jnp.zeros_like(mixed)
+
+    @pl.loop(0, fields)
+    def _(c):
+        square[...] += dot(whole[c], whole[c], 1, 1)
+
+    @pl.loop(0, fields)
+    def _(c):
+        send(c).wait_recv()
+        store(c).start()
+        mixed[...] += dot(whole[c, :, kept], got[c], 1, 1)
+
+    diag[:T] = square[:T, :T]
+    diag[T : 2 * T] = square[T:, :T]
+    diag[2 * T :] = square[T:, T:]
+    lower = jnp.where(mode == 0, mixed[...].T, mixed[...])
+    cross[:T] = lower[:T, :T]
+    cross[T : 2 * T] = lower[:T, T:]
+    cross[2 * T : 3 * T] = lower[T:, :T]
+    cross[3 * T :] = lower[T:, T:]
+    for c in range(fields):
+        store(c).wait()
+        send(c).wait_send()
+
+
+def pair(tensor):
+    rows, fields, cells = tensor.shape
+    any_spec = pl.BlockSpec(memory_space=pl.ANY)
+    vmem = pl.BlockSpec(memory_space=pltpu.VMEM)
+    return pl.pallas_call(
+        pair_kernel,
+        out_shape=[
+            jax.ShapeDtypeStruct((3 * T, T), jnp.float32),
+            jax.ShapeDtypeStruct((4 * T, T), jnp.float32),
+            jax.ShapeDtypeStruct((fields, rows, cells // 2), jnp.float32),
+        ],
+        in_specs=[any_spec],
+        out_specs=[vmem, vmem, any_spec],
+        scratch_shapes=[
+            pltpu.VMEM((fields, rows, cells), jnp.float32),
+            pltpu.VMEM((fields, rows, cells // 2), jnp.float32),
+            pltpu.VMEM((rows, rows), jnp.float32),
+            pltpu.VMEM((rows, rows), jnp.float32),
+        ]
+        + [pltpu.SemaphoreType.DMA((fields,))] * 4,
+        compiler_params=pltpu.CompilerParams(collective_id=1, has_side_effects=True),
+        name="covariance_terms",
+    )(tensor)
+
+
+def project_kernel(
+    basis, tensor, arrived, out, own, theirs, slab, own_sem, their_sem, send_sem, recv_sem, store_sem
+):
+    mode, other = partner()
+    fields, rows, half = own.shape
+    kept = pl.ds(pl.multiple_of(mode * half, T), half)
+    share = out.shape[0]
+
+    def load_own(c):
+        return pltpu.make_async_copy(tensor.at[:, c, kept], own.at[c], own_sem.at[c])
+
+    def load_theirs(c):
+        return pltpu.make_async_copy(arrived.at[c], theirs.at[c], their_sem.at[c])
+
+    def send(c):
+        return pltpu.make_async_remote_copy(
+            src_ref=slab.at[c, 1],
+            dst_ref=out.at[:, c, kept],
+            send_sem=send_sem.at[c],
+            recv_sem=recv_sem.at[c],
+            device_id=other,
+        )
+
+    def store(c):
+        return pltpu.make_async_copy(slab.at[c, 0], out.at[:, c, kept], store_sem.at[c])
+
+    for c in range(fields):
+        load_own(c).start()
+        load_theirs(c).start()
+    greet(other)
+
+    @pl.loop(0, fields)
+    def _(c):
+        load_own(c).wait()
+        load_theirs(c).wait()
+        left = basis[:, pl.ds(pl.multiple_of(mode * rows, T), rows)]
+        right = basis[:, pl.ds(pl.multiple_of((1 - mode) * rows, T), rows)]
+        both = dot(left, own[c], 1, 0) + dot(right, theirs[c], 1, 0)
+        first = mode == 0
+        slab[c, 1] = jnp.where(first, both[share:], both[:share])
+        send(c).start()
+        slab[c, 0] = jnp.where(first, both[:share], both[share:])
+        store(c).start()
+
+    for c in range(fields):
+        store(c).wait()
+        send(c).wait()
+
+
+def project(basis, tensor, arrived):
+    rows, fields, cells = tensor.shape
+    share = basis.shape[0] // 2
+    any_spec = pl.BlockSpec(memory_space=pl.ANY)
+    return pl.pallas_call(
+        project_kernel,
+        out_shape=jax.ShapeDtypeStruct((share, fields, cells), jnp.float32),
+        in_specs=[pl.BlockSpec(memory_space=pltpu.VMEM), any_spec, any_spec],
+        out_specs=any_spec,
+        scratch_shapes=[
+            pltpu.VMEM((fields, rows, cells // 2), jnp.float32),
+            pltpu.VMEM((fields, rows, cells // 2), jnp.float32),
+            pltpu.VMEM((fields, 2, share, cells // 2), jnp.float32),
+        ]
+        + [pltpu.SemaphoreType.DMA((fields,))] * 5,
+        compiler_params=pltpu.CompilerParams(collective_id=2, has_side_effects=True),
+        name="projection",
+    )(basis, tensor, arrived)
+
+
 def local(tensor, start_basis):
-    rows, components, cells = tensor.shape
-    total = components * cells * lax.axis_size("oth")
-    mode = lax.axis_index("mode")
-    swap = [(0, 1), (1, 0)]
-    half = cells // 2
-    away = lax.dynamic_slice_in_dim(tensor, (1 - mode) * half, half, 2)
-    kept = lax.dynamic_slice_in_dim(tensor, mode * half, half, 2)
-    arrived = lax.ppermute(away, "mode", swap)
-    both = (((1, 2), (1, 2)), ((), ()))
-    own = lax.dot_general(tensor, tensor, both, precision=HIGH, preferred_element_type=jnp.float32)
-    mixed = lax.dot_general(kept, arrived, both, precision=HIGH, preferred_element_type=jnp.float32)
-    mixed = jnp.where(mode == 0, mixed.T, mixed)
-    diag = jnp.concatenate([own[:T, :T], own[T:, :T], own[T:, T:]], axis=0)
-    cross = jnp.concatenate([mixed[:T, :T], mixed[:T, T:], mixed[T:, :T], mixed[T:, T:]], axis=0)
+    total = tensor.shape[1] * tensor.shape[2] * lax.axis_size("oth")
+    diag, cross, arrived = pair(tensor)
     sums = summed(diag, cross).reshape(2, -1, T, T)
     triangle, basis = small(1.0 / total, sums, start_basis)
-    rank = basis.shape[1] // 2
-    own_rows = lax.dynamic_slice_in_dim(basis, mode * rows, rows, 0)
-    given = lax.dynamic_slice_in_dim(own_rows, (1 - mode) * rank, rank, 1)
-    mine = lax.dynamic_slice_in_dim(own_rows, mode * rank, rank, 1)
-    first = (((0,), (0,)), ((), ()))
-    sent = lax.ppermute(
-        lax.dot_general(given, tensor, first, precision=HIGH, preferred_element_type=jnp.float32),
-        "mode",
-        swap,
-    )
-    stays = lax.dot_general(mine, tensor, first, precision=HIGH, preferred_element_type=jnp.float32)
-    return (stays + sent, triangle)
+    return (project(basis, tensor, arrived), triangle)
 
 
 def solution(mesh):

time: 223 us -> 99.1 us (0.44)
  Pallas kernels: 161 us -> 95.9 us
  matrix products: 34.6 us -> 0 us
  starting transfers between devices: 11.1 us -> 0 us
  local copies, waits for them, and re-layouts: 11.5 us -> 2.26 us
  waiting for transfers between devices: 2.32 us -> 0 us
    pallas_call x1, Pallas kernels: 122 us -> 33.1 us  [small(): pl.pallas_call(lambda *refs: small_kernel(scale, *refs), out_shape=[jax.S...]
    dot_general x4 -> x0, matrix products: 34.6 us -> none  [the longest x1 16.9 us: local(): lax.dot_general(tensor, tensor, both, precision=HIGH, preferred_element_t...]
    pallas_call x0 -> x2, Pallas kernels: none -> 22.3 us  [the longest x1 15.5 us: pair(): pl.pallas_call(pair_kernel, out_shape=[jax.ShapeDtypeStruct((3 * T, T), j...]
    ppermute x2 -> x0, starting transfers between devices: 11.1 us -> none  [the longest x1 8.91 us: local(): arrived = lax.ppermute(away, 'mode', swap)]
    unnamed x4 -> x1, local copies, waits for them, and re-layouts: 8.21 us -> 2.26 us
    dynamic_slice x1 -> x0, local copies, waits for them, and re-layouts: 3.08 us -> none  [local(): away = lax.dynamic_slice_in_dim(tensor, (1 - mode) * half, half, 2)]
    ppermute x2 -> x0, waiting for transfers between devices: 2.32 us -> none  [the longest x1 2.32 us: local(): lax.ppermute(lax.dot_general(given, tensor, first, precision=HIGH, prefer...]
    pallas_call x1, Pallas kernels: 38.3 us -> 40.5 us  [summed(): pl.pallas_call(sum_kernel, out_shape=jax.ShapeDtypeStruct((2, rows, T), j...]
  transfers between devices with their start and end apart: 2 -> 0, of which waited for: 1 -> 0; matrix products, arithmetic and copies ran while one was open for 8% -> 0% of each run, Pallas kernels for 0% -> 0%
where the time goes in v2:
time: 99.1 us; the launch traced here: 98.8 us
  Pallas kernels  95.9 us (97%)
  local copies, waits for them, and re-layouts  2.26 us (2%)
    pallas_call x1, Pallas kernels, summed(): pl.pallas_call(sum_kernel, out_shape=jax.ShapeDtypeStruct((2, rows, T), j...  40.5 us
    pallas_call x1, Pallas kernels, small(): pl.pallas_call(lambda *refs: small_kernel(scale, *refs), out_shape=[jax.S...  33.1 us
    pallas_call x1, Pallas kernels, pair(): pl.pallas_call(pair_kernel, out_shape=[jax.ShapeDtypeStruct((3 * T, T), j...  15.5 us
    pallas_call x1, Pallas kernels, project(): pl.pallas_call(project_kernel, out_shape=jax.ShapeDtypeStruct((share, fie...  6.85 us
    unnamed x1, local copies, waits for them, and re-layouts  2.26 us

profile of v2, /device:TPU:1, one launch (start us, length us, event | category | flops | bytes accessed | tf_op | source)
XLA Modules:
  0.0 98.8 jit_solution(11040525021432073294)
XLA Ops:
  0.6 15.5 %covariance_terms.1 = (f32[384,128]{1,0:T(8,128)}, f32[512,128]{1,0:T(8,128)}, f32[4,256,512]{2,1,0:T(8,128)}) custom-call(f32[256,4,1024]{2,1,0:T(4,128)} %tensor.3), custom_call_target="tpu_custom_call" | custom-call | tf_op jit(solution)/shard_map/covariance_terms/pallas_call | solution.py:406
  16.1 40.5 %covariance_sum.1 = f32[2,640,128]{2,1,0:T(8,128)} custom-call(f32[384,128]{1,0:T(8,128)} %get-tuple-element.7.diag, f32[512,128]{1,0:T(8,128)} %get-tuple-element.8.cross), custom_call_target="tpu_custom_call" | custom-call | tf_op jit(solution)/shard_map/covariance_sum/pallas_call | solution.py:167
  56.6 33.1 %factors.1 = (f32[512,512]{1,0:T(8,128)}, f32[128,512]{1,0:T(8,128)}) custom-call(f32[2,5,128,128]{3,2,1,0:T(8,128)} %bitcast.1, f32[512,128]{1,0:T(8,128)} %refs_1_.1), custom_call_target="tpu_custom_call" | custom-call | tf_op jit(solution)/shard_map/factors/pallas_call | solution.py:315
  89.7 6.8 %projection.1 = f32[64,4,1024]{2,1,0:T(4,128)} custom-call(f32[128,512]{1,0:T(8,128)} %get-tuple-element.9.basis, f32[256,4,1024]{2,1,0:T(4,128)} %tensor.3, f32[4,256,512]{2,1,0:T(8,128)} %get-tuple-element.10.arrived), custom_call_target="tpu_custom_call" | custom-call | tf_op jit(solution)/shard_map/projection/pallas_call | solution.py:480
  96.5 2.3 %copy.5 = f32[64,4,1024]{2,1,0:T(4,128)} copy(f32[64,4,1024]{2,1,0:T(4,128)} %projection.1) | data formatting | bytes 2097152

commit v3 on v0

v3 whole, which is shorter than its diff:
```python
import jax
import jax.numpy as jnp
from jax import lax
from jax.experimental import pallas as pl
from jax.experimental.pallas import tpu as pltpu
from jax.sharding import PartitionSpec as P

ITERS = 3
T = 128
XS, YS, ZS = 4, 8, 8
HIGH = lax.Precision.HIGHEST


AXES = {"x": XS, "y": YS, "z": ZS}
CHAINS = ((0, 24, "z", "y"), (192, 24, "y", "z"), (384, 16, "z", "y"), (512, 16, "y", "z"))
PER_CHAIN = 40


def dot(a, b, ca, cb):
    return lax.dot_general(
        a, b, (((ca,), (cb,)), ((), ())), precision=HIGH, preferred_element_type=jnp.float32
    )


def covariance_kernel(
    tensor,
    out,
    field,
    whole,
    got,
    square,
    mixed,
    work,
    cross,
    half_in,
    in1,
    in2,
    in3,
    send_sem,
    recv_sem,
    local_sem,
    given_sem,
    taken_sem,
):
    mode = lax.axis_index("mode")
    oth = lax.axis_index("oth")
    x = lax.rem(oth, XS)
    y = lax.rem(oth // XS, YS)
    z = oth // (XS * YS)
    here = {"x": x, "y": y, "z": z}
    other = {"mode": 1 - mode, "oth": oth}
    fields, rows, cells = whole.shape
    half = cells // 2
    kept = pl.ds(pl.multiple_of(mode * half, T), half)
    away = pl.ds(pl.multiple_of((1 - mode) * half, T), half)
    my_rows = pl.ds(pl.multiple_of(mode * rows, T), rows)
    their_rows = pl.ds(pl.multiple_of((1 - mode) * rows, T), rows)

    def along(axis, place):
        spot = dict(here)
        spot[axis] = place
        return {"mode": mode, "oth": (spot["z"] * YS + spot["y"]) * XS + spot["x"]}

    def peer(axis, step):
        return lax.rem(here[axis] + step, AXES[axis])

    def load(c):
        return pltpu.make_async_copy(tensor.at[:, c, :], whole.at[c], local_sem.at[0, c])

    def keep_own(c):
        return pltpu.make_async_copy(whole.at[c], field.at[c, my_rows, :], local_sem.at[1, c])

    def keep_got(c):
        return pltpu.make_async_copy(got.at[c], field.at[c, their_rows, kept], local_sem.at[2, c])

    def give(c):
        return pltpu.make_async_remote_copy(
            src_ref=whole.at[c, :, away],
            dst_ref=got.at[c],
            send_sem=given_sem.at[0, c],
            recv_sem=taken_sem.at[0, c],
            device_id=other,
        )

    def give_rest(c):
        return pltpu.make_async_remote_copy(
            src_ref=whole.at[c, :, kept],
            dst_ref=field.at[c, my_rows, kept],
            send_sem=given_sem.at[1, c],
            recv_sem=taken_sem.at[1, c],
            device_id=other,
        )

    def copy(src, dst, slot, device):
        return pltpu.make_async_remote_copy(
            src_ref=src,
            dst_ref=dst,
            send_sem=send_sem.at[slot],
            recv_sem=recv_sem.at[slot],
            device_id=device,
        )

    for c in range(fields):
        load(c).start()
    barrier = pltpu.get_barrier_semaphore()
    pl.semaphore_signal(barrier, inc=1, device_id=other)
    count = 1
    for axis in "zyx":
        for step in range(1, AXES[axis]):
            pl.semaphore_signal(barrier, inc=1, device_id=along(axis, peer(axis, step)))
            count += 1
    pl.semaphore_wait(barrier, count)

    used = [0]
    started = []

    def launch(src, dst, device):
        item = copy(src, dst, used[0], device)
        used[0] += 1
        item.start()
        started.append(item)
        return item

    def own_rows(chain):
        base, piece, major, minor = CHAINS[chain]
        return pl.ds(pl.multiple_of(base + here[major] * piece, 8), piece)

    def scatter(chain):
        base, piece, major, minor = CHAINS[chain]
        items = []
        for step in range(1, AXES[major]):
            to = peer(major, step)
            part = pl.ds(pl.multiple_of(base + to * piece, 8), piece)
            spot = in1.at[chain, here[major], pl.ds(0, piece)]
            items.append(launch(work.at[part], spot, along(major, to)))
        in1[chain, here[major], :piece] = work[own_rows(chain)]
        return items

    def total(ref, chain, axis):
        piece = CHAINS[chain][1]
        value = ref[chain, 0, :piece]
        for place in range(1, AXES[axis]):
            value = value + ref[chain, place, :piece]
        return value

    def exchange(chain, value, ref, axis):
        piece = CHAINS[chain][1]
        ref[chain, here[axis], :piece] = value
        spot = ref.at[chain, here[axis], pl.ds(0, piece)]
        return [launch(spot, spot, along(axis, peer(axis, step))) for step in range(1, AXES[axis])]

    def arrive(items):
        for item in items:
            item.wait_recv()

    for c in range(fields):
        load(c).wait()
        give(c).start()
    square[...] = jnp.zeros_like(square)
    mixed[...] = jnp.zeros_like(mixed)

    @pl.loop(0, fields)
    def _(c):
        square[...] += dot(whole[c], whole[c], 1, 1)

    work[:T] = square[:T, :T]
    work[T : 2 * T] = square[T:, :T]
    work[2 * T : 3 * T] = square[T:, T:]
    first = {chain: scatter(chain) for chain in (0, 1)}

    @pl.loop(0, fields)
    def _(c):
        give(c).wait_recv()
        mixed[...] += dot(whole[c, :, kept], got[c], 1, 1)

    lower = jnp.where(mode == 0, mixed[...].T, mixed[...])
    cross[:T] = lower[:T, :T]
    cross[T : 2 * T] = lower[:T, T:]
    cross[2 * T : 3 * T] = lower[T:, :T]
    cross[3 * T :] = lower[T:, T:]
    swap = launch(
        cross.at[pl.ds(pl.multiple_of((1 - mode) * 2 * T, 8), 2 * T)], half_in, other
    )
    swap.wait_recv()
    work[3 * T :] = cross[pl.ds(pl.multiple_of(mode * 2 * T, 8), 2 * T)] + half_in[...]
    first.update({chain: scatter(chain) for chain in (2, 3)})
    for c in range(fields):
        give_rest(c).start()
        keep_own(c).start()
        keep_got(c).start()

    second, third, fourth, passed = {}, {}, {}, []
    for chain, (base, piece, major, minor) in enumerate(CHAINS):
        arrive(first[chain])
        second[chain] = exchange(chain, total(in1, chain, major), in2, minor)
    for chain, (base, piece, major, minor) in enumerate(CHAINS):
        arrive(second[chain])
        third[chain] = exchange(chain, total(in2, chain, minor), in3, "x")
    for chain, (base, piece, major, minor) in enumerate(CHAINS):
        arrive(third[chain])
        out[mode, own_rows(chain)] = total(in3, chain, "x")
        spot = out.at[mode, own_rows(chain)]
        fourth[chain] = [
            launch(spot, spot, along(major, peer(major, step))) for step in range(1, AXES[major])
        ]
        passed.append(launch(spot, spot, other))
    for chain, (base, piece, major, minor) in enumerate(CHAINS):
        for step in range(1, AXES[major]):
            fourth[chain][step - 1].wait_recv()
            source = lax.rem(here[major] + (AXES[major] - step), AXES[major])
            spot = out.at[mode, pl.ds(pl.multiple_of(base + source * piece, 8), piece)]
            passed.append(launch(spot, spot, other))
    arrive(passed)
    for item in started:
        item.wait_send()
    for c in range(fields):
        give(c).wait_send()
        give_rest(c).wait()
        keep_own(c).wait()
        keep_got(c).wait()


def covariance(tensor):
    rows, fields, cells = tensor.shape
    any_spec = pl.BlockSpec(memory_space=pl.ANY)
    vmem = pl.BlockSpec(memory_space=pltpu.VMEM)
    count = len(CHAINS)
    most = max(chain[1] for chain in CHAINS)
    copies = 1 + count * PER_CHAIN
    return pl.pallas_call(
        covariance_kernel,
        out_shape=[
            jax.ShapeDtypeStruct((2, 5 * T, T), jnp.float32),
            jax.ShapeDtypeStruct((fields, 2 * rows, cells), jnp.float32),
        ],
        in_specs=[any_spec],
        out_specs=[vmem, any_spec],
        scratch_shapes=[
            pltpu.VMEM((fields, rows, cells), jnp.float32),
            pltpu.VMEM((fields, rows, cells // 2), jnp.float32),
            pltpu.VMEM((rows, rows), jnp.float32),
            pltpu.VMEM((rows, rows), jnp.float32),
            pltpu.VMEM((5 * T, T), jnp.float32),
            pltpu.VMEM((4 * T, T), jnp.float32),
            pltpu.VMEM((2 * T, T), jnp.float32),
            pltpu.VMEM((count, 8, most, T), jnp.float32),
            pltpu.VMEM((count, 8, most, T), jnp.float32),
            pltpu.VMEM((count, XS, most, T), jnp.float32),
            pltpu.SemaphoreType.DMA((copies,)),
            pltpu.SemaphoreType.DMA((copies,)),
            pltpu.SemaphoreType.DMA((3, fields)),
            pltpu.SemaphoreType.DMA((2, fields)),
            pltpu.SemaphoreType.DMA((2, fields)),
        ],
        compiler_params=pltpu.CompilerParams(collective_id=0, has_side_effects=True),
        name="covariance",
    )(tensor)


def thirds(x):
    high = x.astype(jnp.bfloat16).astype(jnp.float32)
    rest = x - high
    middle = rest.astype(jnp.bfloat16).astype(jnp.float32)
    return high, middle, rest - middle


def outer(a, b):
    ah, am, al = thirds(a)
    bh, bm, bl = thirds(b)
    left = jnp.concatenate([ah, ah, am, am, ah, al], axis=0).astype(jnp.bfloat16)
    right = jnp.concatenate([bh, bm, bh, bm, bl, bh], axis=0).astype(jnp.bfloat16)
    return lax.dot_general(
        left, right, (((0,), (0,)), ((), ())), preferred_element_type=jnp.float32
    )


def factor(mats, uppers):
    groups = T // 8
    lane = lax.broadcasted_iota(jnp.int32, (8, T), 1)
    sub = lax.broadcasted_iota(jnp.int32, (8, T), 0)

    def spread(v, i):
        return jnp.broadcast_to(v[i : i + 1, :], (8, T))

    def column(v, i):
        return jnp.broadcast_to(v[:, i : i + 1], (8, T))

    def body(k, state):
        new_state = []
        keep = lane < jnp.where(k == 0, T, T - 8)
        more = k < groups - 1
        active = (lane >= 8) & (lane < T - 8 * k)
        for (mat, left, right), upper in zip(state, uppers):
            mat = list(mat)
            late = outer(left, right)
            for g in range(1, groups - 1):
                mat[g] = jnp.where(keep, mat[g], 0.0) - late[8 * g : 8 * g + 8, :]
            head, following = mat[0], mat[1]
            heads = [column(head, i) for i in range(8)]
            nexts = [jnp.where(more, column(following, i), 0.0) for i in range(8)]
            done = jnp.zeros((8, T), jnp.float32)
            for i in range(8):
                row = spread(head, i)
                inv = lax.rsqrt(spread(heads[i], i))
                square = inv * inv
                at = lane == i
                row_one = jnp.where(at, 1.0, row)
                scaled = row_one * square
                done = jnp.where(sub == i, row * inv, done)
                below = jnp.where(sub > i, heads[i], 0.0)
                for j in range(i + 1, 8):
                    factor_j = spread(heads[j], i) * square
                    heads[j] = heads[j] - below * factor_j
                    nexts[j] = nexts[j] - nexts[i] * factor_j
                head = jnp.where(at, 0.0, head) - below * scaled
                head = jnp.where(sub == i, row_one * inv, head)
                following = jnp.where(at, 0.0, following) - nexts[i] * scaled
            upper[pl.ds(pl.multiple_of(k * 8, 8), 8), :] = pltpu.roll(done, k * 8, axis=1)
            left = jnp.where(active, head, 0.0)
            right = jnp.where((lane < 8) & (lane > sub), 0.0, head)
            mat = [head, following] + mat[2:]
            mat = [pltpu.roll(m, T - 8, axis=1) for m in mat]
            left = pltpu.roll(left, T - 8, axis=1)
            right = pltpu.roll(right, T - 8, axis=1)
            new_state.append((tuple(mat[1:] + mat[:1]), left, right))
        return tuple(new_state)

    zero = jnp.zeros((8, T), jnp.float32)
    state = tuple(
        (tuple(m[8 * g : 8 * g + 8, :] for g in range(groups)), zero, zero) for m in mats
    )
    state = lax.fori_loop(0, groups, body, state)
    row = lax.broadcasted_iota(jnp.int32, (T, T), 0)
    col = lax.broadcasted_iota(jnp.int32, (T, T), 1)
    inverses = [jnp.where(row >= col, jnp.concatenate(s[0], axis=0), 0.0) for s in state]
    lowers = [jnp.where(row <= col, u[...], 0.0).T for u in uppers]
    return lowers, inverses


PLACES = (((0, 0), (1, 0), (1, 1), (2, 0), (2, 1)), ((2, 2), (3, 2), (3, 3), (3, 0), (3, 1)))


def small_kernel(
    scale, sums, start, triangle, basis_turned, covar, work, images, basis, upper1, upper2
):
    blocks = covar.shape[0] // T
    for m in range(2):
        for b, (r, c) in enumerate(PLACES[m]):
            block = sums[m, b] * scale
            covar[r * T : r * T + T, c * T : c * T + T] = block
            work[r * T : r * T + T, c * T : c * T + T] = block
            if r != c:
                covar[c * T : c * T + T, r * T : r * T + T] = block.T
    basis[...] = start[...]
    for r in range(blocks):
        lo = r * T
        mats = [work[lo : lo + T, lo : lo + T]]
        uppers = [upper1]
        if r < ITERS:
            images[...] = dot(covar[...], basis[...], 1, 0)
            mats.append(dot(images[...], images[...], 0, 0))
            uppers.append(upper2)
        lowers, inverses = factor(mats, uppers)
        triangle[lo : lo + T, lo : lo + T] = lowers[0]
        if r < ITERS - 1:
            basis[...] = dot(images[...], inverses[1], 1, 1)
        elif r == ITERS - 1:
            basis_turned[...] = dot(inverses[1], images[...], 1, 1)
        if r > 0:
            triangle[:lo, lo : lo + T] = jnp.zeros((lo, T), jnp.float32)
        if r < blocks - 1:
            panel = dot(work[lo + T :, lo : lo + T], inverses[0], 1, 1)
            triangle[lo + T :, lo : lo + T] = panel
            for c in range(r + 1, blocks):
                top = c * T
                work[top:, top : top + T] = work[top:, top : top + T] - dot(
                    panel[top - lo - T :, :], panel[top - lo - T : top - lo, :], 1, 1
                )


def small(scale, sums, start_basis):
    n, rank = start_basis.shape
    return pl.pallas_call(
        lambda *refs: small_kernel(scale, *refs),
        out_shape=[
            jax.ShapeDtypeStruct((n, n), jnp.float32),
            jax.ShapeDtypeStruct((rank, n), jnp.float32),
        ],
        in_specs=[pl.BlockSpec(memory_space=pltpu.VMEM)] * 2,
        out_specs=[pl.BlockSpec(memory_space=pltpu.VMEM)] * 2,
        scratch_shapes=[
            pltpu.VMEM((n, n), jnp.float32),
            pltpu.VMEM((n, n), jnp.float32),
            pltpu.VMEM((n, rank), jnp.float32),
            pltpu.VMEM((n, rank), jnp.float32),
            pltpu.VMEM((T, T), jnp.float32),
            pltpu.VMEM((T, T), jnp.float32),
        ],
        name="factors",
    )(sums, start_basis)


def project_kernel(basis, field, out, block, slab, load_sem, store_sem):
    fields, share = slab.shape[:2]
    mine = basis[pl.ds(pl.multiple_of(lax.axis_index("mode") * share, 8), share), :]

    def load(c):
        return pltpu.make_async_copy(field.at[c], block.at[c], load_sem.at[c])

    def store(c):
        return pltpu.make_async_copy(slab.at[c], out.at[:, c, :], store_sem.at[c])

    for c in range(fields):
        load(c).start()
    for c in range(fields):
        load(c).wait()
        slab[c] = dot(mine, block[c], 1, 0)
        store(c).start()
    for c in range(fields):
        store(c).wait()


def project(basis, field):
    fields, rows, cells = field.shape
    share = basis.shape[0] // 2
    any_spec = pl.BlockSpec(memory_space=pl.ANY)
    return pl.pallas_call(
        project_kernel,
        out_shape=jax.ShapeDtypeStruct((share, fields, cells), jnp.float32),
        in_specs=[pl.BlockSpec(memory_space=pltpu.VMEM), any_spec],
        out_specs=any_spec,
        scratch_shapes=[
            pltpu.VMEM((fields, rows, cells), jnp.float32),
            pltpu.VMEM((fields, share, cells), jnp.float32),
            pltpu.SemaphoreType.DMA((fields,)),
            pltpu.SemaphoreType.DMA((fields,)),
        ],
        name="projection",
    )(basis, field)


def local(tensor, start_basis):
    total = tensor.shape[1] * tensor.shape[2] * lax.axis_size("oth")
    sums, field = covariance(tensor)
    triangle, basis = small(1.0 / total, sums.reshape(2, -1, T, T), start_basis)
    return (project(basis, field), triangle)


def solution(mesh):
    return jax.shard_map(
        local,
        mesh=mesh,
        in_specs=(P("mode", None, "oth"), P()),
        out_specs=(P("mode", None, "oth"), P()),
        check_vma=False,
    )
```

time: 651 us -> 90.5 us (0.14); the launches traced: 643 us -> 90.3 us
  waiting for transfers between devices: 379 us -> 0 us
  other arithmetic: 149 us -> 0 us
  Pallas kernels: 0 us -> 89.5 us
  local copies, waits for them, and re-layouts: 39.7 us -> 0 us
  matrix products: 28.3 us -> 0 us
  blocking collectives: 18.3 us -> 0 us
  between operations: 17 us -> 0.8 us
  starting transfers between devices: 11.8 us -> 0 us
    unnamed x4 -> x0, waiting for transfers between devices: 275 us -> none
    another operation x29 -> x0, other arithmetic: 148 us -> none  [the longest x14 78.8 us: local(): triangle = jnp.linalg.cholesky(summed_covar)]
    pallas_call x0 -> x3, Pallas kernels: none -> 89.5 us  [the longest x1 47.9 us: covariance(): pl.pallas_call(covariance_kernel, out_shape=[jax.ShapeDtypeStruct((2, 5 *...]
    all_gather x1 -> x0, waiting for transfers between devices: 86.7 us -> none  [local(): lax.all_gather(summed_piece, ('mode', 'oth'), axis=0, tiled=True)]
    dot_general x11 -> x0, matrix products: 25.2 us -> none  [the longest x1 7.79 us: local(): lax.dot_general(own_rows, local_unfolded, (((0,), (0,)), ((), ())), preci...]
    unnamed x10 -> x0, local copies, waits for them, and re-layouts: 24.1 us -> none
    all_to_all x1 -> x0, blocking collectives: 18.3 us -> none  [local(): lax.all_to_all(tensor, 'mode', split_axis=2, concat_axis=0, tiled=True)]
    reduce_scatter x1 -> x0, waiting for transfers between devices: 17.3 us -> none  [local(): lax.psum_scatter(product.reshape(lax.axis_size('mode') * (rank_total // g...]
  transfers between devices with their start and end apart: 3 -> 0, of which waited for: 3 -> 0; matrix products, arithmetic and copies ran while one was open for 2% -> 0% of each run, Pallas kernels for 0% -> 0%
where the time goes in v3:
time: 90.5 us; the launch traced here: 90.3 us
  Pallas kernels  89.5 us (99%)
    pallas_call x1, Pallas kernels, covariance(): pl.pallas_call(covariance_kernel, out_shape=[jax.ShapeDtypeStruct((2, 5 *...  47.9 us
    pallas_call x1, Pallas kernels, small(): pl.pallas_call(lambda *refs: small_kernel(scale, *refs), out_shape=[jax.S...  33.2 us
    pallas_call x1, Pallas kernels, project(): pl.pallas_call(project_kernel, out_shape=jax.ShapeDtypeStruct((share, fie...  8.44 us

profile of v3, /device:TPU:1, one launch (start us, length us, event | category | flops | bytes accessed | tf_op | source)
XLA Modules:
  0.0 90.3 jit_solution(2103052083721699745)
XLA Ops:
  0.6 47.9 %covariance.1 = (f32[2,640,128]{2,1,0:T(8,128)}, f32[4,512,1024]{2,1,0:T(8,128)}) custom-call(f32[256,4,1024]{2,1,0:T(4,128)} %tensor.1), custom_call_target="tpu_custom_call" | custom-call | tf_op jit(solution)/shard_map/covariance/pallas_call | solution.py:230
  48.5 33.2 %factors.1 = (f32[512,512]{1,0:T(8,128)}, f32[128,512]{1,0:T(8,128)}) custom-call(f32[2,5,128,128]{3,2,1,0:T(8,128)} %bitcast.1, f32[512,128]{1,0:T(8,128)} %refs_1_.1), custom_call_target="tpu_custom_call" | custom-call | tf_op jit(solution)/shard_map/factors/pallas_call | solution.py:383
  81.7 8.4 %projection.1 = f32[64,4,1024]{2,1,0:T(4,128)} custom-call(f32[128,512]{1,0:T(8,128)} %get-tuple-element.7.basis, f32[4,512,1024]{2,1,0:T(8,128)} %get-tuple-element.8.field), custom_call_target="tpu_custom_call" | custom-call | tf_op jit(solution)/shard_map/projection/pallas_call | solution.py:427

commit v4 on v3

--- a/solution.py
+++ b/solution.py
@@ -285,54 +285,51 @@
     def column(v, i):
         return jnp.broadcast_to(v[:, i : i + 1], (8, T))
 
-    def body(k, state):
-        new_state = []
-        keep = lane < jnp.where(k == 0, T, T - 8)
-        more = k < groups - 1
-        active = (lane >= 8) & (lane < T - 8 * k)
-        for (mat, left, right), upper in zip(state, uppers):
-            mat = list(mat)
-            late = outer(left, right)
-            for g in range(1, groups - 1):
-                mat[g] = jnp.where(keep, mat[g], 0.0) - late[8 * g : 8 * g + 8, :]
-            head, following = mat[0], mat[1]
-            heads = [column(head, i) for i in range(8)]
-            nexts = [jnp.where(more, column(following, i), 0.0) for i in range(8)]
+    states = [[[m[8 * g : 8 * g + 8, :] for g in range(groups)], None, None] for m in mats]
+    for k in range(groups):
+        first = 8 * k
+        for state, upper in zip(states, uppers):
+            mat, left, right = state
+            if k > 0:
+                late = outer(left, right)
+                before = (lane >= first - 8) & (lane < first)
+                for g in range(k + 1, groups):
+                    mat[g] = jnp.where(before, 0.0, mat[g]) - late[8 * g : 8 * g + 8, :]
+            last = k == groups - 1
+            head = mat[k]
+            heads = [column(head, first + i) for i in range(8)]
+            if not last:
+                following = mat[k + 1]
+                nexts = [column(following, first + i) for i in range(8)]
             done = jnp.zeros((8, T), jnp.float32)
             for i in range(8):
                 row = spread(head, i)
                 inv = lax.rsqrt(spread(heads[i], i))
                 square = inv * inv
-                at = lane == i
+                at = lane == first + i
                 row_one = jnp.where(at, 1.0, row)
                 scaled = row_one * square
                 done = jnp.where(sub == i, row * inv, done)
                 below = jnp.where(sub > i, heads[i], 0.0)
                 for j in range(i + 1, 8):
-                    factor_j = spread(heads[j], i) * square
-                    heads[j] = heads[j] - below * factor_j
-                    nexts[j] = nexts[j] - nexts[i] * factor_j
+                    entry = spread(heads[j], i)
+                    heads[j] = heads[j] - (below * entry) * square
+                    if not last:
+                        nexts[j] = nexts[j] - nexts[i] * (entry * square)
                 head = jnp.where(at, 0.0, head) - below * scaled
                 head = jnp.where(sub == i, row_one * inv, head)
-                following = jnp.where(at, 0.0, following) - nexts[i] * scaled
-            upper[pl.ds(pl.multiple_of(k * 8, 8), 8), :] = pltpu.roll(done, k * 8, axis=1)
-            left = jnp.where(active, head, 0.0)
-            right = jnp.where((lane < 8) & (lane > sub), 0.0, head)
-            mat = [head, following] + mat[2:]
-            mat = [pltpu.roll(m, T - 8, axis=1) for m in mat]
-            left = pltpu.roll(left, T - 8, axis=1)
-            right = pltpu.roll(right, T - 8, axis=1)
-            new_state.append((tuple(mat[1:] + mat[:1]), left, right))
-        return tuple(new_state)
-
-    zero = jnp.zeros((8, T), jnp.float32)
-    state = tuple(
-        (tuple(m[8 * g : 8 * g + 8, :] for g in range(groups)), zero, zero) for m in mats
-    )
-    state = lax.fori_loop(0, groups, body, state)
+                if not last:
+                    following = jnp.where(at, 0.0, following) - nexts[i] * scaled
+            upper[first : first + 8, :] = done
+            state[1] = jnp.where(lane >= first + 8, head, 0.0)
+            inside = (lane >= first) & (lane < first + 8) & (lane - first > sub)
+            state[2] = jnp.where(inside, 0.0, head)
+            mat[k] = head
+            if not last:
+                mat[k + 1] = following
     row = lax.broadcasted_iota(jnp.int32, (T, T), 0)
     col = lax.broadcasted_iota(jnp.int32, (T, T), 1)
-    inverses = [jnp.where(row >= col, jnp.concatenate(s[0], axis=0), 0.0) for s in state]
+    inverses = [jnp.where(row >= col, jnp.concatenate(s[0], axis=0), 0.0) for s in states]
     lowers = [jnp.where(row <= col, u[...], 0.0).T for u in uppers]
     return lowers, inverses
 
@@ -412,9 +409,17 @@
 
     for c in range(fields):
         load(c).start()
+    high = mine.astype(jnp.bfloat16)
+    low = (mine - high.astype(jnp.float32)).astype(jnp.bfloat16)
+    stacked = jnp.concatenate([high, low], axis=0)
     for c in range(fields):
         load(c).wait()
-        slab[c] = dot(mine, block[c], 1, 0)
+        values = block[c]
+        main = values.astype(jnp.bfloat16)
+        rest = (values - main.astype(jnp.float32)).astype(jnp.bfloat16)
+        wide = jnp.dot(stacked, main, preferred_element_type=jnp.float32)
+        thin = jnp.dot(high, rest, preferred_element_type=jnp.float32)
+        slab[c] = wide[:share] + (wide[share:] + thin)
         store(c).start()
     for c in range(fields):
         store(c).wait()

time: 90.5 us -> 83.6 us (0.924)
  Pallas kernels: 89.5 us -> 82.6 us
    pallas_call x1, Pallas kernels: 33.2 us -> 28.9 us  [small(): pl.pallas_call(lambda *refs: small_kernel(scale, *refs), out_shape=[jax.S...]
    pallas_call x1, Pallas kernels: 8.44 us -> 5.82 us  [project(): pl.pallas_call(project_kernel, out_shape=jax.ShapeDtypeStruct((share, fie...]
where the time goes in v4:
time: 83.6 us; the launch traced here: 83.4 us
  Pallas kernels  82.6 us (99%)
    pallas_call x1, Pallas kernels, covariance(): pl.pallas_call(covariance_kernel, out_shape=[jax.ShapeDtypeStruct((2, 5 *...  47.9 us
    pallas_call x1, Pallas kernels, small(): pl.pallas_call(lambda *refs: small_kernel(scale, *refs), out_shape=[jax.S...  28.9 us
    pallas_call x1, Pallas kernels, project(): pl.pallas_call(project_kernel, out_shape=jax.ShapeDtypeStruct((share, fie...  5.82 us

profile of v4, /device:TPU:1, one launch (start us, length us, event | category | flops | bytes accessed | tf_op | source)
XLA Modules:
  0.0 83.4 jit_solution(12022238376016975008)
XLA Ops:
  0.6 47.9 %covariance.1 = (f32[2,640,128]{2,1,0:T(8,128)}, f32[4,512,1024]{2,1,0:T(8,128)}) custom-call(f32[256,4,1024]{2,1,0:T(4,128)} %tensor.1), custom_call_target="tpu_custom_call" | custom-call | tf_op jit(solution)/shard_map/covariance/pallas_call | solution.py:230
  48.5 28.9 %factors.1 = (f32[512,512]{1,0:T(8,128)}, f32[128,512]{1,0:T(8,128)}) custom-call(f32[2,5,128,128]{3,2,1,0:T(8,128)} %bitcast.1, f32[512,128]{1,0:T(8,128)} %refs_1_.1), custom_call_target="tpu_custom_call" | custom-call | tf_op jit(solution)/shard_map/factors/pallas_call | solution.py:380
  77.5 5.8 %projection.1 = f32[64,4,1024]{2,1,0:T(4,128)} custom-call(f32[128,512]{1,0:T(8,128)} %get-tuple-element.7.basis, f32[4,512,1024]{2,1,0:T(8,128)} %get-tuple-element.8.field), custom_call_target="tpu_custom_call" | custom-call | tf_op jit(solution)/shard_map/projection/pallas_call | solution.py:432
